TPU v7x, 32 devices: a whole 2x2x4 slice. The times are simulated.
32 devices in a mesh: freq: 8 (over z, y), tm: 4 (over x, core).
Axes of the slice: x: 2, y: 2, z: 4, core: 2. Of those that a mesh axis runs over, the one named last changes fastest.
Arguments:
- voltages: float32 [8, 2, 32, 16384], P('freq', None, None, 'tm'), as said below
- local_delay: int32 [128, 32], P('freq'), may hold values from 0 to 15
- merge_table: int32 [3, 3, 128], P(None, None, 'freq'), may hold values from 0 to 32, as said below
- box_widths: int32 [4], replicated, may hold values from 1 to 32, as said below
Outputs:
- detection: float32 [128, 4, 16384], P('freq', None, 'tm')
Inputs may be any that keep to these rules, and one draw needn't show every extreme that they name: `voltages`: finite real and imaginary parts. `merge_table`: for each level l and each band's 16 output trials, entries 0 and 1 are each a permutation of 0 .. 15; entry 2 lies in 0 .. 8 * 2^l and equals that bound for some trial of every level. `box_widths`: the last width is 32.
All inputs are finite; a program needn't handle non-finite values.
Results may differ from a plain program's by a relative error of at most 0.0001.
Values sent between devices are 32-bit elements; how exact they have to be, the bound alone decides.
No kernel may reach another device: no remote copies, remote signals or barrier semaphores. Data moves between devices by JAX's collectives and lax.ppermute only.
A program may use at most 64 MiB of HBM per device.

v0:
```python
import functools
import math

import jax
import jax.numpy as jnp
from jax import lax
from jax.experimental import pallas as pl
from jax.experimental.pallas import tpu as pltpu
from jax.sharding import PartitionSpec as P

TAPS = 4
LOCAL_MAX = 16
SHIFT_UNIT = 8
WMAX = 32
LANES = 128
OUT_COPIES = 2
FETCHES = 2
UNIT = 2
SHARES = (19, 8, 6)
PIECES = len(SHARES)
STREAMED = 3

epsilon = 1e-06

VM = pl.BlockSpec(memory_space=pltpu.VMEM)
SM = pl.BlockSpec(memory_space=pltpu.SMEM)
HBM = pl.BlockSpec(memory_space=pltpu.HBM)
PARAMS = pltpu.CompilerParams(vmem_limit_bytes=16 << 20)
SOURCE_LIMIT = 55_500_000
F32 = jnp.float32
BF16 = jnp.bfloat16


def swapped(value, axis, mask):
    pairs = [(source, source ^ mask) for source in range(lax.axis_size(axis))]
    return lax.ppermute(value, axis, pairs)


def shifted(block, axis, distance):
    devices = range(lax.axis_size(axis))
    route = [(i - distance, i) for i in devices if i - distance in devices]
    return lax.ppermute(block, axis, route)


def window_columns(branches):
    shape = (branches, LANES)
    place = (lane_index(shape) % TAPS * branches + row_index(shape)).astype(F32)
    length = TAPS * branches
    offset = (place - length / 2 + 0.5) * (math.pi / branches)
    hamming = 0.54 - 0.46 * jnp.cos(place * (2.0 * math.pi / (length - 1)))
    return jnp.sin(offset) / offset * hamming


def fourier_rows(branches):
    shape = (2 * branches, 4 * branches)
    row, column = row_index(shape), lane_index(shape)
    quarter = branches // 4
    turn = (row % branches) * (column % branches)
    turn = turn + jnp.where(row >= branches, 2 * quarter, quarter)
    turn = turn - jnp.where(column % (2 * branches) >= branches, quarter, 0)
    turn = turn % branches
    negative = turn > 2 * quarter
    turn = jnp.where(negative, turn - 2 * quarter, turn)
    turn = jnp.where(turn > quarter, 2 * quarter - turn, turn)
    value = jnp.zeros(shape, F32)
    for step in range(1, quarter + 1):
        value = jnp.where(turn == step, math.sin(2.0 * math.pi * step / branches), value)
    return jnp.where(negative, -value, value)


def halves(x):
    high = x.astype(BF16)
    return high, (x - high.astype(F32)).astype(BF16)


def thirds(x):
    high = x.astype(BF16)
    rest = x - high.astype(F32)
    middle = rest.astype(BF16)
    return high, middle, (rest - middle.astype(F32)).astype(BF16)


def lane_index(shape):
    return lax.broadcasted_iota(jnp.int32, shape, len(shape) - 1)


def row_index(shape):
    return lax.broadcasted_iota(jnp.int32, shape, 0)


def channel_kernel(
    pieces, x_hbm, power_ref, small_ref, big_ref, x_ref, win_ref, w_ref, sems
):
    rows, time_count = x_ref.shape
    branches = rows // 2
    width = time_count // pieces
    edge = TAPS - 1
    copies = []
    for piece in range(pieces):
        part = pl.ds(piece * width, width)
        copies.append(pltpu.make_async_copy(x_hbm.at[:, part], x_ref.at[:, part], sems.at[piece]))
        copies[-1].start()
    window = window_columns(branches)
    for tap in range(TAPS):
        column = jnp.broadcast_to(window[:, tap : tap + 1], (branches, LANES))
        win_ref[tap, :branches] = column
        win_ref[tap, branches:] = column
    w_ref[...] = jnp.concatenate(halves(fourier_rows(branches)), axis=1)

    group = 16
    lane = lane_index((group, LANES))
    nothing = jnp.zeros((group, LANES), F32)
    memory = [(nothing, nothing)] * (rows // group)
    total = jnp.zeros((branches, LANES), F32)
    tiles = time_count // LANES
    for tile in range(0, tiles + 1, UNIT):
        if tile < tiles and tile * LANES % width == 0:
            copies[tile * LANES // width].wait()
        unit = range(tile, min(tile + UNIT, tiles + 1))
        parts = {0: [], 1: []}
        for index in range(rows // group):
            part = slice(index * group, (index + 1) * group)
            older, sum_older = memory[index]
            row = {0: [], 1: []}
            for number in unit:
                if number < tiles:
                    here = x_ref[part, number * LANES : (number + 1) * LANES]
                    moved = pltpu.roll(here, 2, 1)
                    twice = jnp.where(lane < 2, older, moved)
                    even = win_ref[3, part] * here + win_ref[1, part] * twice
                    odd = win_ref[2, part] * here + win_ref[0, part] * twice
                else:
                    moved = nothing
                    twice = jnp.where(lane < 2, older, 0.0)
                    even = win_ref[1, part] * twice
                    odd = win_ref[0, part] * twice
                sum_moved = pltpu.roll(odd, 1, 1)
                filtered = even + jnp.where(lane < 1, sum_older, sum_moved)
                older, sum_older = moved, sum_moved
                for half, value in enumerate(halves(filtered)):
                    row[half].append(value)
            memory[index] = (older, sum_older)
            for half in range(2):
                parts[half].append(jnp.concatenate(row[half], axis=1))
        stack = jnp.concatenate(parts[0] + parts[1], axis=0)
        spectra = jnp.dot(
            w_ref[...], jnp.concatenate([stack, stack], axis=0), preferred_element_type=F32
        )
        for number in unit:
            value = spectra[:, (number - tile) * LANES : (number - tile + 1) * LANES]
            if number == 0:
                own = value
            if number == tiles:
                following = value
                continue
            power = value[:branches] ** 2 + value[branches:] ** 2
            power_ref[:, number * LANES : (number + 1) * LANES] = power
            if number == 0:
                power = jnp.where(lane_index(power.shape) >= edge, power, 0.0)
            total = total + power
    sums = jnp.sum(total, axis=1, keepdims=True)
    sums = jnp.concatenate([sums, jnp.zeros_like(sums)], axis=0)
    lane = lane_index((rows, LANES))
    packed = jnp.where(lane == 2 * edge, sums, 0.0)
    packed = jnp.where(lane < 2 * edge, pltpu.roll(own, edge, 1), packed)
    packed = jnp.where(lane < edge, following, packed)
    packed = jnp.concatenate([packed, jnp.zeros((LANES - rows, LANES), F32)], axis=0)
    packet = jnp.transpose(packed)[:8]
    small_ref[...] = packet
    big_ref[:8] = packet
    big_ref[8:] = power


def channelize(samples, pieces):
    rows, time_count = samples.shape
    branches = rows // 2
    return pl.pallas_call(
        functools.partial(channel_kernel, pieces),
        in_specs=[HBM],
        out_specs=[VM] * 3,
        out_shape=[
            jax.ShapeDtypeStruct((branches, time_count), F32),
            jax.ShapeDtypeStruct((8, LANES), F32),
            jax.ShapeDtypeStruct((8 + branches, LANES), F32),
        ],
        scratch_shapes=[
            pltpu.VMEM((rows, time_count), F32),
            pltpu.VMEM((TAPS, rows, LANES), F32),
            pltpu.VMEM((rows, 4 * rows), BF16),
            pltpu.SemaphoreType.DMA((pieces,)),
        ],
        compiler_params=pltpu.CompilerParams(vmem_limit_bytes=SOURCE_LIMIT),
        name="channelize",
    )(samples)


FINE = 2
PARTS = 3


def trial_rows(selector, trials, value, value_before, products_before):
    joined = jnp.concatenate([value_before, value], axis=1)
    stack = []
    for lag in range(FINE):
        moved = pltpu.roll(joined, lag, 1)[:, LANES:] if lag else value
        stack.extend(thirds(moved))
    products = jnp.dot(selector, jnp.concatenate(stack, axis=0), preferred_element_type=F32)
    rows = products[:trials]
    for step in range(1, LOCAL_MAX // FINE):
        part = slice(step * trials, (step + 1) * trials)
        both = jnp.concatenate([products_before[part], products[part]], axis=1)
        rows = rows + pltpu.roll(both, FINE * step, 1)[:, LANES:]
    width = value.shape[1]
    return rows, value[:, width - LANES :], products[:, width - LANES :]


def first_rows_kernel(peers, time_all, *refs):
    power_ref, packets, selector_ref = refs[0], refs[1 : 1 + peers], refs[1 + peers]
    rows_ref, scale_ref, line_ref, fold_ref = refs[2 + peers :]
    branches = power_ref.shape[0]
    trials = rows_ref.shape[0]
    rank = lax.axis_index("tm")
    edge = TAPS - 1

    line_ref[:8] = jnp.zeros((8, LANES), F32)
    for peer in range(peers):
        spot = pl.multiple_of(((rank ^ peer) + 1) * 8, 8)
        line_ref[pl.ds(spot, 8), :] = packets[peer][:8]
    mine = line_ref[8:]
    amplitude = mine + pltpu.roll(line_ref[: 8 * peers], edge, 0)
    square = amplitude * amplitude
    folded = square + pltpu.roll(square, LANES - branches, 1)
    fold_ref[...] = folded
    kind = row_index(mine.shape) % 8
    whole = jnp.where(kind == 2 * edge, mine, 0.0)
    whole = jnp.where((kind >= edge) & (kind < 2 * edge), folded, whole)
    band_mean = jnp.sum(whole, axis=0, keepdims=True) / time_all
    scale = 1.0 / (band_mean + epsilon)
    firsts = fold_ref[pl.ds(pl.multiple_of(rank * 8, 8), 8), :]
    firsts = jnp.where(row_index(firsts.shape) == 2 * edge, scale, firsts)
    columns = jnp.transpose(firsts)[:branches]
    scale = jnp.broadcast_to(columns[:, 2 * edge : 2 * edge + 1], (branches, LANES))
    scale_ref[...] = scale
    scale = scale[:, :1]

    tail = jnp.zeros((branches, LANES), F32)
    for peer in range(1, peers):
        if peer & (peer + 1) == 0:
            tail = jnp.where((rank ^ (rank - 1)) == peer, packets[peer][8:], tail)
    halo = jnp.where(rank > 0, tail * scale - 1.0, 0.0)
    start = power_ref[:, :LANES]
    for lane in range(edge):
        value = columns[:, edge + lane : edge + lane + 1]
        start = jnp.where(lane_index(start.shape) == lane, value, start)

    selector = selector_ref[...]
    width = rows_ref.shape[1] - LANES
    value = jnp.concatenate([start, power_ref[:, LANES:width]], axis=1) * scale - 1.0
    value = jnp.concatenate([halo, value], axis=1)
    nothing = jnp.zeros((selector.shape[0], LANES), F32)
    rows_ref[...], _, _ = trial_rows(selector, trials, value, jnp.zeros_like(halo), nothing)


def first_rows(power, packets, selector, tiles, time_all):
    branches = power.shape[0]
    trials = selector.shape[0] * FINE // LOCAL_MAX
    peers = len(packets)
    return pl.pallas_call(
        functools.partial(first_rows_kernel, peers, time_all),
        in_specs=[VM] * (2 + peers),
        out_specs=[VM] * 2,
        out_shape=[
            jax.ShapeDtypeStruct((trials, tiles * LANES), F32),
            jax.ShapeDtypeStruct((branches, LANES), F32),
        ],
        scratch_shapes=[
            pltpu.VMEM((8 * (peers + 1), LANES), F32),
            pltpu.VMEM((8 * peers, LANES), F32),
        ],
        compiler_params=PARAMS,
        name="first_rows",
    )(power, *packets, selector)


def more_rows_kernel(start, power_ref, scale_ref, selector_ref, rows_ref):
    trials, width = rows_ref.shape
    scale = scale_ref[:, :1]
    value = power_ref[:, start - LANES : start + width] * scale - 1.0
    selector = selector_ref[...]
    nothing = jnp.zeros((selector.shape[0], LANES), F32)
    rows, _, _ = trial_rows(selector, trials, value, jnp.zeros_like(value[:, :LANES]), nothing)
    rows_ref[...] = rows[:, LANES:]


def more_rows(power, scale, selector, start, tiles):
    trials = selector.shape[0] * FINE // LOCAL_MAX
    return pl.pallas_call(
        functools.partial(more_rows_kernel, start),
        in_specs=[VM] * 3,
        out_specs=VM,
        out_shape=jax.ShapeDtypeStruct((trials, tiles * LANES), F32),
        compiler_params=PARAMS,
        name="more_rows",
    )(power, scale, selector)


def delayed_rows(rows, amount):
    lane = lane_index(amount.shape)
    source = (lane - amount) & (LANES - 1)
    tiles = [
        jnp.take_along_axis(rows[:, start : start + LANES], source, axis=1)
        for start in range(0, rows.shape[1], LANES)
    ]
    moved = [jnp.where(lane < amount, old, new) for old, new in zip(tiles, tiles[1:])]
    return jnp.concatenate(moved, axis=1)


def merged(level, first, refs):
    pick_ref, amount_ref, own_ref, their_ref = refs[:4]
    trials = own_ref.shape[0]
    if first:
        before = jnp.zeros((trials, LANES), F32)
        own = jnp.concatenate([before, own_ref[...]], axis=1)
        their = jnp.concatenate([before, their_ref[...]], axis=1)
    else:
        own = jnp.concatenate([refs[4][:, refs[4].shape[1] - LANES :], own_ref[...]], axis=1)
        their = jnp.concatenate([refs[5][:, refs[5].shape[1] - LANES :], their_ref[...]], axis=1)
    pick = pick_ref[2 * trials * level : 2 * trials * (level + 1)]
    amount = amount_ref[trials * level : trials * (level + 1)]
    stack = jnp.concatenate(thirds(jnp.concatenate([own, their], axis=0)), axis=0)
    picked = jnp.dot(pick, stack, preferred_element_type=F32)
    return picked[:trials, LANES:] + delayed_rows(picked[trials:], amount)


def merge_kernel(level, first, *refs):
    refs[-1][...] = merged(level, first, refs[:-1])


def merge(level, table, own, their, before):
    return pl.pallas_call(
        functools.partial(merge_kernel, level, not before),
        in_specs=[VM] * (4 + len(before)),
        out_specs=VM,
        out_shape=jax.ShapeDtypeStruct(own.shape, F32),
        compiler_params=PARAMS,
        name="merge",
    )(*table, own, their, *before)


def tables_kernel(divisor, width_ref, delay_ref, table_ref, after_ref, *refs):
    del after_ref
    selector_ref, mask_ref, factor_ref, pick_ref, amount_ref = refs
    trials, channels = delay_ref.shape
    depth = FINE * PARTS * channels
    spread = row_index((channels, depth)) == lane_index((channels, depth)) % channels
    wanted = jnp.dot(
        delay_ref[...].astype(BF16), spread.astype(BF16), preferred_element_type=F32
    ).astype(jnp.int32)
    offset = lane_index((trials, depth)) // (PARTS * channels)
    coarse = LOCAL_MAX // FINE
    selector = jnp.concatenate(
        [(wanted == offset + FINE * step).astype(F32) for step in range(coarse)], axis=0
    ).astype(BF16)
    selector_ref[...] = selector

    shape = (2 * LANES, LANES)
    back = lane_index(shape) + LANES - row_index(shape)
    boxes = width_ref.shape[0]
    wide = jnp.ones(factor_ref.shape, jnp.int32)
    for box in range(boxes):
        inside = (back >= 0) & (back < width_ref[box])
        mask_ref[:, box * LANES : (box + 1) * LANES] = inside.astype(F32).astype(BF16)
        wide = jnp.where(row_index(wide.shape) == box, width_ref[box], wide)
    factor_ref[...] = 1.0 / (jnp.sqrt(wide.astype(F32)) * divisor)
    entries = table_ref[...].astype(jnp.int32)
    column = lane_index((trials, 2 * trials))
    for level in range(amount_ref.shape[0] // trials):
        upper = (lax.axis_index("freq") >> level) & 1
        low = entries[:, 3 * level : 3 * level + 1] + upper * trials
        high = entries[:, 3 * level + 1 : 3 * level + 2] + (1 - upper) * trials
        pick = jnp.concatenate([column == low, column == high], axis=0).astype(F32)
        pick = jnp.concatenate([pick] * 3, axis=1).astype(BF16)
        pick_ref[2 * trials * level : 2 * trials * (level + 1)] = pick
        amount = entries[:, 3 * level + 2 : 3 * level + 3]
        amount_ref[trials * level : trials * (level + 1)] = jnp.broadcast_to(amount, (trials, LANES))


def tables(widths, delays, entries, levels, divisor, after):
    boxes = widths.shape[0]
    trials, channels = delays.shape
    return pl.pallas_call(
        functools.partial(tables_kernel, divisor),
        in_specs=[SM, VM, VM, VM],
        out_specs=[VM] * 5,
        out_shape=[
            jax.ShapeDtypeStruct((LOCAL_MAX // FINE * trials, FINE * PARTS * channels), BF16),
            jax.ShapeDtypeStruct((2 * LANES, boxes * LANES), BF16),
            jax.ShapeDtypeStruct((-(-boxes // 8) * 8, LANES), F32),
            jax.ShapeDtypeStruct((2 * trials * levels, 6 * trials), BF16),
            jax.ShapeDtypeStruct((trials * levels, LANES), jnp.int32),
        ],
        compiler_params=PARAMS,
        name="tables",
    )(widths, delays, entries, after)


def boxcar_pieces(rows, mask_ref, factor_ref, out_ref, begin, end):
    boxes, trials, _ = out_ref.shape
    pairs = [rows[:, tile * LANES : (tile + 2) * LANES] for tile in range(begin, end)]
    high, low = halves(jnp.concatenate(pairs, axis=0))
    mask = mask_ref[...]
    sums = jnp.dot(high, mask, preferred_element_type=F32)
    sums = sums + jnp.dot(low, mask, preferred_element_type=F32)
    for box in range(boxes):
        factor = factor_ref[box : box + 1]
        for tile in range(begin, end):
            line = slice((tile - begin) * trials, (tile - begin + 1) * trials)
            value = sums[line, box * LANES : (box + 1) * LANES] * factor
            out_ref[box, :, tile * LANES : (tile + 1) * LANES] = value


def detect_kernel(level, first, *refs):
    mask_ref, factor_ref = refs[2:4]
    rows_ref, out_ref = refs[-2:]
    rows = merged(level, first, (*refs[:2], *refs[4:8]))
    rows_ref[...] = rows
    if not first:
        before = refs[8]
        rows = jnp.concatenate([before[:, before.shape[1] - LANES :], rows], axis=1)
    boxcar_pieces(rows, mask_ref, factor_ref, out_ref, 0, out_ref.shape[2] // LANES)


def detect(level, table, masks, own, their, before):
    trials, width = own.shape
    operands = [*table, *masks, own, their, *before]
    boxes = masks[0].shape[1] // LANES
    if not before:
        width = width - LANES
    return pl.pallas_call(
        functools.partial(detect_kernel, level, not before),
        in_specs=[VM] * len(operands),
        out_specs=[VM] * 2,
        out_shape=[
            jax.ShapeDtypeStruct(own.shape, F32),
            jax.ShapeDtypeStruct((boxes, trials, width), F32),
        ],
        compiler_params=PARAMS,
        name="detect",
    )(*operands)


def finish_kernel(level, *refs):
    mask_ref, factor_ref = refs[2:4]
    before, ready = refs[8], refs[9:-3]
    out_hbm, out_ref, sem = refs[-3:]
    boxes = out_ref.shape[0]
    copies = []

    def write(source, box, begin, end, start):
        number = len(copies)
        copies.append(
            pltpu.make_async_copy(
                source.at[box, :, pl.ds(begin, end - begin)],
                out_hbm.at[:, box, pl.ds(start + begin, end - begin)],
                sem.at[number],
            )
        )
        copies[-1].start()

    start = 0
    for piece in ready:
        for box in range(boxes):
            write(piece, box, 0, piece.shape[2], start)
        start += piece.shape[2]
    rows = merged(level, False, (*refs[:2], *refs[4:8]))
    rows = jnp.concatenate([before[:, before.shape[1] - LANES :], rows], axis=1)
    tiles = out_ref.shape[2] // LANES
    bounds = [tiles * part // OUT_COPIES for part in range(OUT_COPIES + 1)]
    for begin, end in zip(bounds, bounds[1:]):
        boxcar_pieces(rows, mask_ref, factor_ref, out_ref, begin, end)
        for box in range(boxes):
            write(out_ref, box, begin * LANES, end * LANES, start)
    for copy in copies:
        copy.wait()


def finish(level, table, masks, own, their, before, ready):
    trials, width = own.shape
    operands = [*table, *masks, own, their, *before, *ready]
    boxes = masks[0].shape[1] // LANES
    time_count = width + sum(piece.shape[2] for piece in ready)
    return pl.pallas_call(
        functools.partial(finish_kernel, level),
        in_specs=[VM] * len(operands),
        out_specs=HBM,
        out_shape=jax.ShapeDtypeStruct((trials, boxes, time_count), F32),
        scratch_shapes=[
            pltpu.VMEM((boxes, trials, width), F32),
            pltpu.SemaphoreType.DMA((boxes * (len(ready) + OUT_COPIES),)),
        ],
        compiler_params=PARAMS,
        name="finish",
    )(*operands)


def selector_rows(chosen, row_count):
    return (chosen[:, None] == jnp.arange(row_count, dtype=jnp.int32)[None, :]).astype(F32)


def delay_rows(picked_high, delay_amount, delay_reach):
    current = picked_high
    for bit_index in range(delay_reach.bit_length()):
        step_size = 2**bit_index
        moved = jnp.concatenate(
            [
                jnp.zeros((current.shape[0], step_size), F32),
                current[:, : current.shape[1] - step_size],
            ],
            axis=1,
        )
        bit_set = (jnp.right_shift(delay_amount, bit_index) % 2 == 1)[:, None]
        current = jnp.where(bit_set, moved, current)
    return current[:, delay_reach:]


def merge_level(own_rows, their_rows, level_table, is_upper, delay_reach):
    lower_rows = jnp.where(is_upper, their_rows, own_rows)
    upper_rows = jnp.where(is_upper, own_rows, their_rows)
    row_count = own_rows.shape[0]
    pick = functools.partial(jnp.dot, precision=lax.Precision.HIGHEST, preferred_element_type=F32)
    picked_low = pick(selector_rows(level_table[0], row_count), lower_rows[:, delay_reach:])
    picked_high = pick(selector_rows(level_table[1], row_count), upper_rows)
    return picked_low + delay_rows(picked_high, level_table[2], delay_reach)


def boxcar(dedispersed, widths):
    time_count = dedispersed.shape[1] - (WMAX - 1)
    detection = jnp.zeros((dedispersed.shape[0], widths.shape[0], time_count), F32)
    for offset in range(WMAX):
        width_mask = (offset < widths).astype(F32)
        lagged = dedispersed[:, WMAX - 1 - offset : WMAX - 1 - offset + time_count]
        detection = detection + lagged[:, None, :] * width_mask[None, :, None]
    return detection / jnp.sqrt(widths.astype(F32))[None, :, None]


def body(voltages, local_delay, merge_table, box_widths):
    branches = voltages.shape[2]
    time_count = voltages.shape[3]
    freq_size = lax.axis_size("freq")
    tm_size = lax.axis_size("tm")
    level_count = freq_size.bit_length() - 1
    streamed = min(STREAMED, level_count)
    trials = local_delay.shape[0]
    divisor = math.sqrt(branches * freq_size)

    power, small, big = channelize(voltages.reshape(2 * branches, time_count), FETCHES)
    packets = [small]
    for peer in range(1, tm_size):
        packets.append(swapped(big if peer & (peer + 1) == 0 else small, "tm", peer))

    entries = merge_table[:streamed].reshape(3 * streamed, trials).T.astype(F32)
    entries = jnp.pad(entries, ((0, 0), (0, LANES - 3 * streamed)))
    tiles = 1 + time_count // LANES
    sizes = [tiles * share // sum(SHARES) for share in SHARES]
    sizes[-1] += tiles - sum(sizes)
    starts = [sum(sizes[:i]) * LANES - LANES for i in range(len(sizes))]
    selector, mask, factor, *table = tables(
        box_widths, local_delay, entries, streamed, divisor, small
    )
    masks = (mask, factor)
    rows, scale = first_rows(power, packets, selector, sizes[0], float(time_count * tm_size))
    pieces = [rows]
    for i in range(1, PIECES):
        pieces.append(more_rows(power, scale, selector, starts[i], sizes[i]))

    for level in range(streamed):
        their = []
        for piece in pieces:
            their.append(swapped(piece, "freq", 2**level))
        results = []
        ready = []
        for i in range(PIECES):
            before = [pieces[i - 1], their[i - 1]] if i else []
            if level < level_count - 1:
                results.append(merge(level, table, pieces[i], their[i], before))
                continue
            if i:
                before.append(results[i - 1])
            if i == PIECES - 1:
                return finish(level, table, masks, pieces[i], their[i], before, ready)
            rows, boxed = detect(level, table, masks, pieces[i], their[i], before)
            results.append(rows)
            ready.append(boxed)
        pieces = results
    freq_rank = lax.axis_index("freq")
    dm_rows = jnp.concatenate(pieces, axis=1)[:, LANES:]
    for level_index in range(streamed, level_count):
        delay_reach = SHIFT_UNIT * 2**level_index
        tail_rows = shifted(dm_rows[:, time_count - delay_reach :], "tm", 1)
        own_rows = jnp.concatenate([tail_rows, dm_rows], axis=1)
        their_rows = swapped(own_rows, "freq", 2**level_index)
        is_upper = jnp.right_shift(freq_rank, level_index) % 2 == 1
        dm_rows = merge_level(own_rows, their_rows, merge_table[level_index], is_upper, delay_reach)
    tail_rows = shifted(dm_rows[:, time_count - (WMAX - 1) :], "tm", 1)
    return boxcar(jnp.concatenate([tail_rows, dm_rows], axis=1) / divisor, box_widths)


def solution(mesh):
    return jax.shard_map(
        body,
        mesh=mesh,
        in_specs=(P("freq", None, None, "tm"), P("freq", None), P(None, None, "freq"), P()),
        out_specs=P("freq", None, "tm"),
        check_vma=False,
    )
```

profile of v0, /device:TPU:0, one launch (start us, length us, event | category | flops | bytes accessed | tf_op | source)
XLA Modules:
  0.0 40.7 jit_solution(6045467830601462309)
XLA Ops:
  0.0 0.0 copy-start.2
  0.0 2.4 %channelize.1 = (f32[32,4096]{1,0:T(8,128)S(1)}, f32[8,128]{1,0:T(8,128)S(1)}, f32[40,128]{1,0:T(8,128)S(1)}) custom-call(f32[64,4096]{1,0:T(8,128)} %bitcast.2), custom_call_target="tpu_custom_call" | custom-call | tf_op jit(solution)/shard_map/channelize/pallas_call | solution.py:177
  2.4 2.5 %collective-permute-start.2 = (f32[40,128]{1,0:T(8,128)S(1)}, f32[40,128]{1,0:T(8,128)S(1)}, u32[]{:S(2)}, u32[]{:S(2)}) collective-permute-start(f32[40,128]{1,0:T(8,128)S(1)} %get-tuple-element.25), channel_id=1, source_target_pairs={{0,3},{1,2},{2,1},{3,0},{4,7},{5,6},{6,5},{7,4},{8,11},{9,10},{10,... | collective-permute-start | bytes 61448 | tf_op jit(solution)/shard_map/ppermute | solution.py:36
  4.9 0.7 %collective-permute-start = (f32[40,128]{1,0:T(8,128)S(1)}, f32[40,128]{1,0:T(8,128)S(1)}, u32[]{:S(2)}, u32[]{:S(2)}) collective-permute-start(f32[40,128]{1,0:T(8,128)S(1)} %get-tuple-element.25), channel_id=1, source_target_pairs={{0,1},{1,0},{2,3},{3,2},{4,5},{5,4},{6,7},{7,6},{8,9},{9,8},{10,11... | collective-permute-start | bytes 61448 | tf_op jit(solution)/shard_map/ppermute | solution.py:36
  5.6 0.0 collective-permute-start.1
  5.6 0.0 copy-done.2
  5.6 0.1 copy.6
  5.7 0.0 copy-start
  5.7 0.0 copy-start.1
  5.7 0.7 %copy-done = s32[16,32]{1,0:T(8,128)S(1)} copy-done((s32[16,32]{1,0:T(8,128)S(1)}, s32[16,32]{1,0:T(8,128)}, u32[]{:S(2)}) %copy-start) | copy-done | bytes 2072
  6.4 0.0 copy-done.1
  6.4 0.8 %tables.1 = (bf16[128,192]{1,0:T(8,128)(2,1)S(1)}, bf16[256,512]{1,0:T(8,128)(2,1)S(1)}, f32[8,128]{1,0:T(8,128)S(1)}, bf16[96,96]{1,0:T(8,128)(2,1)S(1)}, s32[48,128]{1,0:T(8,128)S(1)}) custom-call(s32[4]{0:T(128)S(1)} %copy-done.1, s32[16,32]{1,0:T(8,128)S(1)} %copy-done, f32[16,128]{1,0:T(8,128)S(1)} %pad.4.table_ref, ...), custom_call_target="tpu_custom_call" | custom-call | tf_op jit(solution)/shard_map/tables/pallas_call | solution.py:391
  7.2 2.0 %collective-permute-done.1.refs_3_ = f32[8,128]{1,0:T(8,128)S(1)} collective-permute-done((f32[8,128]{1,0:T(8,128)S(1)}, f32[8,128]{1,0:T(8,128)S(1)}, u32[]{:S(2)}, u32[]{:S(2)}) %collective-permute-start.1) | collective-permute-done | bytes 4128 | tf_op jit(solution)/shard_map/ppermute | solution.py:36
  9.2 0.0 collective-permute-done.2.refs_4_
  9.2 0.0 collective-permute-done.refs_2_
  9.2 0.9 %first_rows.1 = (f32[16,2432]{1,0:T(8,128)S(1)}, f32[32,128]{1,0:T(8,128)S(1)}) custom-call(f32[32,4096]{1,0:T(8,128)S(1)} %get-tuple-element.24.refs_0_.power_ref, f32[8,128]{1,0:T(8,128)S(1)} %get-tuple-element.19.after_ref.refs_1_, f32[40,128]{1,0:T(8,128)S(1)} %collective-permute-done.refs_2_, f32[8,128]{1,0:T(8,128)S(1)} %collective-permute-done.1.refs_3_, ...), custom_call_target="tpu_custom_call" | custom-call | tf_op jit(solution)/shard_map/first_rows/pallas_call | solution.py:268
  10.1 1.6 %collective-permute-start.6 = (f32[16,2432]{1,0:T(8,128)S(1)}, f32[16,2432]{1,0:T(8,128)S(1)}, u32[]{:S(2)}, u32[]{:S(2)}) collective-permute-start(f32[16,2432]{1,0:T(8,128)S(1)} %get-tuple-element.28.refs_4_.refs_2_), channel_id=1, source_target_pairs={{0,4},{4,0},{8,12},{12,8},{16,20},{20,16},{24,28},{28,24},{1,5},{5... | collective-permute-start | bytes 466952 | tf_op jit(solution)/shard_map/ppermute | solution.py:36
  11.7 3.7 %collective-permute-done.6.refs_5_.refs_3_ = f32[16,2432]{1,0:T(8,128)S(1)} collective-permute-done((f32[16,2432]{1,0:T(8,128)S(1)}, f32[16,2432]{1,0:T(8,128)S(1)}, u32[]{:S(2)}, u32[]{:S(2)}) %collective-permute-start.6) | collective-permute-done | bytes 155680 | tf_op jit(solution)/shard_map/ppermute | solution.py:36
  15.4 0.3 merge.9.refs_4_.refs_2_
  15.6 1.6 %collective-permute-start.9 = (f32[16,2432]{1,0:T(8,128)S(1)}, f32[16,2432]{1,0:T(8,128)S(1)}, u32[]{:S(2)}, u32[]{:S(2)}) collective-permute-start(f32[16,2432]{1,0:T(8,128)S(1)} %merge.9.refs_4_.refs_2_), channel_id=1, source_target_pairs={{0,8},{4,12},{8,0},{12,4},{16,24},{20,28},{24,16},{28,20},{1,9},{5... | collective-permute-start | bytes 466952 | tf_op jit(solution)/shard_map/ppermute | solution.py:36
  17.3 0.5 %more_rows.3.refs_4_.refs_2_ = f32[16,1024]{1,0:T(8,128)S(1)} custom-call(f32[32,4096]{1,0:T(8,128)S(1)} %get-tuple-element.24.refs_0_.power_ref, f32[32,128]{1,0:T(8,128)S(1)} %get-tuple-element.27.scale_ref, bf16[128,192]{1,0:T(8,128)(2,1)S(1)} %get-tuple-element.26.refs_5_.selector_ref), custom_call_target="tpu_custom_call" | custom-call | tf_op jit(solution)/shard_map/more_rows/pallas_call | solution.py:297
  17.8 1.6 %collective-permute-start.4 = (f32[16,1024]{1,0:T(8,128)S(1)}, f32[16,1024]{1,0:T(8,128)S(1)}, u32[]{:S(2)}, u32[]{:S(2)}) collective-permute-start(f32[16,1024]{1,0:T(8,128)S(1)} %more_rows.3.refs_4_.refs_2_), channel_id=1, source_target_pairs={{0,4},{4,0},{8,12},{12,8},{16,20},{20,16},{24,28},{28,24},{1,5},{5... | collective-permute-start | bytes 196616 | tf_op jit(solution)/shard_map/ppermute | solution.py:36
  19.4 1.6 %collective-permute-done.9.refs_5_.refs_3_ = f32[16,2432]{1,0:T(8,128)S(1)} collective-permute-done((f32[16,2432]{1,0:T(8,128)S(1)}, f32[16,2432]{1,0:T(8,128)S(1)}, u32[]{:S(2)}, u32[]{:S(2)}) %collective-permute-start.9) | collective-permute-done | bytes 155680 | tf_op jit(solution)/shard_map/ppermute | solution.py:36
  20.9 0.3 merge.11.refs_4_.refs_6_
  21.2 3.3 %collective-permute-start.11 = (f32[16,2432]{1,0:T(8,128)S(1)}, f32[16,2432]{1,0:T(8,128)S(1)}, u32[]{:S(2)}, u32[]{:S(2)}) collective-permute-start(f32[16,2432]{1,0:T(8,128)S(1)} %merge.11.refs_4_.refs_6_), channel_id=1, source_target_pairs={{0,16},{4,20},{8,24},{12,28},{16,0},{20,4},{24,8},{28,12},{1,17},{... | collective-permute-start | bytes 466952 | tf_op jit(solution)/shard_map/ppermute | solution.py:36
  24.5 0.5 %more_rows.2.refs_2_ = f32[16,768]{1,0:T(8,128)S(1)} custom-call(f32[32,4096]{1,0:T(8,128)S(1)} %get-tuple-element.24.refs_0_.power_ref, f32[32,128]{1,0:T(8,128)S(1)} %get-tuple-element.27.scale_ref, bf16[128,192]{1,0:T(8,128)(2,1)S(1)} %get-tuple-element.26.refs_5_.selector_ref), custom_call_target="tpu_custom_call" | custom-call | tf_op jit(solution)/shard_map/more_rows/pallas_call | solution.py:297
  25.0 1.6 %collective-permute-start.3 = (f32[16,768]{1,0:T(8,128)S(1)}, f32[16,768]{1,0:T(8,128)S(1)}, u32[]{:S(2)}, u32[]{:S(2)}) collective-permute-start(f32[16,768]{1,0:T(8,128)S(1)} %more_rows.2.refs_2_), channel_id=1, source_target_pairs={{0,4},{4,0},{8,12},{12,8},{16,20},{20,16},{24,28},{28,24},{1,5},{5... | collective-permute-start | bytes 147464 | tf_op jit(solution)/shard_map/ppermute | solution.py:36
  26.5 0.0 collective-permute-done.4.refs_5_.refs_3_
  26.5 0.2 merge.7.refs_4_.refs_2_
  26.8 1.0 %collective-permute-start.7 = (f32[16,1024]{1,0:T(8,128)S(1)}, f32[16,1024]{1,0:T(8,128)S(1)}, u32[]{:S(2)}, u32[]{:S(2)}) collective-permute-start(f32[16,1024]{1,0:T(8,128)S(1)} %merge.7.refs_4_.refs_2_), channel_id=1, source_target_pairs={{0,8},{4,12},{8,0},{12,4},{16,24},{20,28},{24,16},{28,20},{1,9},{5... | collective-permute-start | bytes 196616 | tf_op jit(solution)/shard_map/ppermute | solution.py:36
  27.8 1.3 %collective-permute-done.3.refs_3_ = f32[16,768]{1,0:T(8,128)S(1)} collective-permute-done((f32[16,768]{1,0:T(8,128)S(1)}, f32[16,768]{1,0:T(8,128)S(1)}, u32[]{:S(2)}, u32[]{:S(2)}) %collective-permute-start.3) | collective-permute-done | bytes 49184 | tf_op jit(solution)/shard_map/ppermute | solution.py:36
  29.1 0.2 merge.6.refs_2_
  29.3 1.0 %collective-permute-start.5 = (f32[16,768]{1,0:T(8,128)S(1)}, f32[16,768]{1,0:T(8,128)S(1)}, u32[]{:S(2)}, u32[]{:S(2)}) collective-permute-start(f32[16,768]{1,0:T(8,128)S(1)} %merge.6.refs_2_), channel_id=1, source_target_pairs={{0,8},{4,12},{8,0},{12,4},{16,24},{20,28},{24,16},{28,20},{1,9},{5... | collective-permute-start | bytes 147464 | tf_op jit(solution)/shard_map/ppermute | solution.py:36
  30.4 0.8 %collective-permute-done.7.refs_5_.refs_3_ = f32[16,1024]{1,0:T(8,128)S(1)} collective-permute-done((f32[16,1024]{1,0:T(8,128)S(1)}, f32[16,1024]{1,0:T(8,128)S(1)}, u32[]{:S(2)}, u32[]{:S(2)}) %collective-permute-start.7) | collective-permute-done | bytes 65568 | tf_op jit(solution)/shard_map/ppermute | solution.py:36
  31.1 0.2 merge.10.refs_4_.refs_6_
  31.4 0.5 %collective-permute-start.10 = (f32[16,1024]{1,0:T(8,128)S(1)}, f32[16,1024]{1,0:T(8,128)S(1)}, u32[]{:S(2)}, u32[]{:S(2)}) collective-permute-start(f32[16,1024]{1,0:T(8,128)S(1)} %merge.10.refs_4_.refs_6_), channel_id=1, source_target_pairs={{0,16},{4,20},{8,24},{12,28},{16,0},{20,4},{24,8},{28,12},{1,17},{... | collective-permute-start | bytes 196616 | tf_op jit(solution)/shard_map/ppermute | solution.py:36
  31.8 1.7 %collective-permute-done.5.refs_3_ = f32[16,768]{1,0:T(8,128)S(1)} collective-permute-done((f32[16,768]{1,0:T(8,128)S(1)}, f32[16,768]{1,0:T(8,128)S(1)}, u32[]{:S(2)}, u32[]{:S(2)}) %collective-permute-start.5) | collective-permute-done | bytes 49184 | tf_op jit(solution)/shard_map/ppermute | solution.py:36
  33.5 0.2 merge.8.refs_4_
  33.7 0.9 %collective-permute-start.8 = (f32[16,768]{1,0:T(8,128)S(1)}, f32[16,768]{1,0:T(8,128)S(1)}, u32[]{:S(2)}, u32[]{:S(2)}) collective-permute-start(f32[16,768]{1,0:T(8,128)S(1)} %merge.8.refs_4_), channel_id=1, source_target_pairs={{0,16},{4,20},{8,24},{12,28},{16,0},{20,4},{24,8},{28,12},{1,17},{... | collective-permute-start | bytes 147464 | tf_op jit(solution)/shard_map/ppermute | solution.py:36
  34.7 0.0 collective-permute-done.11.refs_5_.refs_7_
  34.7 0.5 %detect.2 = (f32[16,2432]{1,0:T(8,128)S(1)}, f32[4,16,2304]{2,1,0:T(8,128)S(1)}) custom-call(bf16[96,96]{1,0:T(8,128)(2,1)S(1)} %get-tuple-element.20.refs_0_, s32[48,128]{1,0:T(8,128)S(1)} %get-tuple-element.21.refs_1_, bf16[256,512]{1,0:T(8,128)(2,1)S(1)} %get-tuple-element.22.refs_2_, f32[8,128]{1,0:T(8,128)S(1)} %get-tuple-element.23.refs_3_, ...), custom_call_target="tpu_custom_call" | custom-call | tf_op jit(solution)/shard_map/detect/pallas_call | solution.py:439
  35.2 1.4 %collective-permute-done.10.refs_5_.refs_7_ = f32[16,1024]{1,0:T(8,128)S(1)} collective-permute-done((f32[16,1024]{1,0:T(8,128)S(1)}, f32[16,1024]{1,0:T(8,128)S(1)}, u32[]{:S(2)}, u32[]{:S(2)}) %collective-permute-start.10) | collective-permute-done | bytes 65568 | tf_op jit(solution)/shard_map/ppermute | solution.py:36
  36.6 0.4 %detect.3 = (f32[16,1024]{1,0:T(8,128)S(1)}, f32[4,16,1024]{2,1,0:T(8,128)S(1)}) custom-call(bf16[96,96]{1,0:T(8,128)(2,1)S(1)} %get-tuple-element.20.refs_0_, s32[48,128]{1,0:T(8,128)S(1)} %get-tuple-element.21.refs_1_, bf16[256,512]{1,0:T(8,128)(2,1)S(1)} %get-tuple-element.22.refs_2_, f32[8,128]{1,0:T(8,128)S(1)} %get-tuple-element.23.refs_3_, ...), custom_call_target="tpu_custom_call" | custom-call | tf_op jit(solution)/shard_map/detect/pallas_call | solution.py:439
  37.0 2.3 %collective-permute-done.8.refs_5_ = f32[16,768]{1,0:T(8,128)S(1)} collective-permute-done((f32[16,768]{1,0:T(8,128)S(1)}, f32[16,768]{1,0:T(8,128)S(1)}, u32[]{:S(2)}, u32[]{:S(2)}) %collective-permute-start.8) | collective-permute-done | bytes 49184 | tf_op jit(solution)/shard_map/ppermute | solution.py:36
  39.3 1.4 %finish.1 = f32[16,4,4096]{2,1,0:T(4,128)} custom-call(bf16[96,96]{1,0:T(8,128)(2,1)S(1)} %get-tuple-element.20.refs_0_, s32[48,128]{1,0:T(8,128)S(1)} %get-tuple-element.21.refs_1_, bf16[256,512]{1,0:T(8,128)(2,1)S(1)} %get-tuple-element.22.refs_2_, f32[8,128]{1,0:T(8,128)S(1)} %get-tuple-element.23.refs_3_, f32[16,768]{1,0:T(8,128)S(1)} %merge.8.refs_4_, ...), custom_call_target="tpu_custom_call" | custom-call | tf_op jit(solution)/shard_map/finish/pallas_call | solution.py:492
  (3 shorter events, 0.0 us)
Async XLA Ops:
  0.0 5.6 %copy-start.2 = (s32[3,3,16]{2,1,0:T(4,128)S(1)}, s32[3,3,16]{2,1,0:T(4,128)}, u32[]{:S(2)}) copy-start(s32[3,3,16]{2,1,0:T(4,128)} %param.6) | copy-start | bytes 1732
  2.4 6.8 %collective-permute-start.2 = (f32[40,128]{1,0:T(8,128)S(1)}, f32[40,128]{1,0:T(8,128)S(1)}, u32[]{:S(2)}, u32[]{:S(2)}) collective-permute-start(f32[40,128]{1,0:T(8,128)S(1)} %get-tuple-element.25), channel_id=1, source_target_pairs={{0,3},{1,2},{2,1},{3,0},{4,7},{5,6},{6,5},{7,4},{8,11},{9,10},{10,... | collective-permute-start | bytes 61448 | tf_op jit(solution)/shard_map/ppermute | solution.py:36
  4.9 4.3 %collective-permute-start = (f32[40,128]{1,0:T(8,128)S(1)}, f32[40,128]{1,0:T(8,128)S(1)}, u32[]{:S(2)}, u32[]{:S(2)}) collective-permute-start(f32[40,128]{1,0:T(8,128)S(1)} %get-tuple-element.25), channel_id=1, source_target_pairs={{0,1},{1,0},{2,3},{3,2},{4,5},{5,4},{6,7},{7,6},{8,9},{9,8},{10,11... | collective-permute-start | bytes 61448 | tf_op jit(solution)/shard_map/ppermute | solution.py:36
  5.6 3.6 %collective-permute-start.1 = (f32[8,128]{1,0:T(8,128)S(1)}, f32[8,128]{1,0:T(8,128)S(1)}, u32[]{:S(2)}, u32[]{:S(2)}) collective-permute-start(f32[8,128]{1,0:T(8,128)S(1)} %get-tuple-element.19.after_ref.refs_1_), channel_id=1, source_target_pairs={{0,2},{1,3},{2,0},{3,1},{4,6},{5,7},{6,4},{7,5},{8,10},{9,11},{10,... | collective-permute-start | bytes 12296 | tf_op jit(solution)/shard_map/ppermute | solution.py:36
  5.7 0.7 %copy-start = (s32[16,32]{1,0:T(8,128)S(1)}, s32[16,32]{1,0:T(8,128)}, u32[]{:S(2)}) copy-start(s32[16,32]{1,0:T(8,128)} %delay_ref.1) | copy-start | bytes 6148
  5.7 0.7 %copy-start.1 = (s32[4]{0:T(128)S(1)}, s32[4]{0:T(128)}, u32[]{:S(2)}) copy-start(s32[4]{0:T(128)} %width_ref.1) | copy-start | bytes 52
  10.1 5.3 %collective-permute-start.6 = (f32[16,2432]{1,0:T(8,128)S(1)}, f32[16,2432]{1,0:T(8,128)S(1)}, u32[]{:S(2)}, u32[]{:S(2)}) collective-permute-start(f32[16,2432]{1,0:T(8,128)S(1)} %get-tuple-element.28.refs_4_.refs_2_), channel_id=1, source_target_pairs={{0,4},{4,0},{8,12},{12,8},{16,20},{20,16},{24,28},{28,24},{1,5},{5... | collective-permute-start | bytes 466952 | tf_op jit(solution)/shard_map/ppermute | solution.py:36
  15.6 5.3 %collective-permute-start.9 = (f32[16,2432]{1,0:T(8,128)S(1)}, f32[16,2432]{1,0:T(8,128)S(1)}, u32[]{:S(2)}, u32[]{:S(2)}) collective-permute-start(f32[16,2432]{1,0:T(8,128)S(1)} %merge.9.refs_4_.refs_2_), channel_id=1, source_target_pairs={{0,8},{4,12},{8,0},{12,4},{16,24},{20,28},{24,16},{28,20},{1,9},{5... | collective-permute-start | bytes 466952 | tf_op jit(solution)/shard_map/ppermute | solution.py:36
  17.8 8.8 %collective-permute-start.4 = (f32[16,1024]{1,0:T(8,128)S(1)}, f32[16,1024]{1,0:T(8,128)S(1)}, u32[]{:S(2)}, u32[]{:S(2)}) collective-permute-start(f32[16,1024]{1,0:T(8,128)S(1)} %more_rows.3.refs_4_.refs_2_), channel_id=1, source_target_pairs={{0,4},{4,0},{8,12},{12,8},{16,20},{20,16},{24,28},{28,24},{1,5},{5... | collective-permute-start | bytes 196616 | tf_op jit(solution)/shard_map/ppermute | solution.py:36
  21.2 13.4 %collective-permute-start.11 = (f32[16,2432]{1,0:T(8,128)S(1)}, f32[16,2432]{1,0:T(8,128)S(1)}, u32[]{:S(2)}, u32[]{:S(2)}) collective-permute-start(f32[16,2432]{1,0:T(8,128)S(1)} %merge.11.refs_4_.refs_6_), channel_id=1, source_target_pairs={{0,16},{4,20},{8,24},{12,28},{16,0},{20,4},{24,8},{28,12},{1,17},{... | collective-permute-start | bytes 466952 | tf_op jit(solution)/shard_map/ppermute | solution.py:36
  25.0 4.2 %collective-permute-start.3 = (f32[16,768]{1,0:T(8,128)S(1)}, f32[16,768]{1,0:T(8,128)S(1)}, u32[]{:S(2)}, u32[]{:S(2)}) collective-permute-start(f32[16,768]{1,0:T(8,128)S(1)} %more_rows.2.refs_2_), channel_id=1, source_target_pairs={{0,4},{4,0},{8,12},{12,8},{16,20},{20,16},{24,28},{28,24},{1,5},{5... | collective-permute-start | bytes 147464 | tf_op jit(solution)/shard_map/ppermute | solution.py:36
  26.8 4.3 %collective-permute-start.7 = (f32[16,1024]{1,0:T(8,128)S(1)}, f32[16,1024]{1,0:T(8,128)S(1)}, u32[]{:S(2)}, u32[]{:S(2)}) collective-permute-start(f32[16,1024]{1,0:T(8,128)S(1)} %merge.7.refs_4_.refs_2_), channel_id=1, source_target_pairs={{0,8},{4,12},{8,0},{12,4},{16,24},{20,28},{24,16},{28,20},{1,9},{5... | collective-permute-start | bytes 196616 | tf_op jit(solution)/shard_map/ppermute | solution.py:36
  29.3 4.2 %collective-permute-start.5 = (f32[16,768]{1,0:T(8,128)S(1)}, f32[16,768]{1,0:T(8,128)S(1)}, u32[]{:S(2)}, u32[]{:S(2)}) collective-permute-start(f32[16,768]{1,0:T(8,128)S(1)} %merge.6.refs_2_), channel_id=1, source_target_pairs={{0,8},{4,12},{8,0},{12,4},{16,24},{20,28},{24,16},{28,20},{1,9},{5... | collective-permute-start | bytes 147464 | tf_op jit(solution)/shard_map/ppermute | solution.py:36
  31.4 5.2 %collective-permute-start.10 = (f32[16,1024]{1,0:T(8,128)S(1)}, f32[16,1024]{1,0:T(8,128)S(1)}, u32[]{:S(2)}, u32[]{:S(2)}) collective-permute-start(f32[16,1024]{1,0:T(8,128)S(1)} %merge.10.refs_4_.refs_6_), channel_id=1, source_target_pairs={{0,16},{4,20},{8,24},{12,28},{16,0},{20,4},{24,8},{28,12},{1,17},{... | collective-permute-start | bytes 196616 | tf_op jit(solution)/shard_map/ppermute | solution.py:36
  33.7 5.6 %collective-permute-start.8 = (f32[16,768]{1,0:T(8,128)S(1)}, f32[16,768]{1,0:T(8,128)S(1)}, u32[]{:S(2)}, u32[]{:S(2)}) collective-permute-start(f32[16,768]{1,0:T(8,128)S(1)} %merge.8.refs_4_), channel_id=1, source_target_pairs={{0,16},{4,20},{8,24},{12,28},{16,0},{20,4},{24,8},{28,12},{1,17},{... | collective-permute-start | bytes 147464 | tf_op jit(solution)/shard_map/ppermute | solution.py:36
where the time goes:
time: 40.9 us; the launch traced here: 40.7 us
  starting transfers between devices  16.3 us (40%)
  waiting for transfers between devices  14.7 us (36%)
  Pallas kernels  8.78 us (21%)
  local copies, waits for them, and re-layouts  0.8 us (2%)
    ppermute x12, starting transfers between devices, swapped(): return lax.ppermute(value, axis, pairs)  16.3 us
    ppermute x12, waiting for transfers between devices, swapped(): return lax.ppermute(value, axis, pairs)  14.7 us
    pallas_call x1, Pallas kernels, channelize(): pl.pallas_call(functools.partial(channel_kernel, pieces), in_specs=[HBM],...  2.42 us
    pallas_call x6, Pallas kernels, merge(): pl.pallas_call(functools.partial(merge_kernel, level, not before), in_spe...  1.45 us
    pallas_call x1, Pallas kernels, finish(): pl.pallas_call(functools.partial(finish_kernel, level), in_specs=[VM] * l...  1.37 us
    pallas_call x2, Pallas kernels, more_rows(): pl.pallas_call(functools.partial(more_rows_kernel, start), in_specs=[VM]...  0.98 us
    pallas_call x2, Pallas kernels, detect(): pl.pallas_call(functools.partial(detect_kernel, level, not before), in_sp...  0.94 us
    pallas_call x1, Pallas kernels, first_rows(): pl.pallas_call(functools.partial(first_rows_kernel, peers, time_all), in_...  0.86 us
  transfers between devices with their start and end apart: 12, of which 8 were waited for; matrix products, arithmetic and copies ran while one was open for 0% of the time, Pallas kernels for 9%

commit v1 on v0

--- a/solution.py
+++ b/solution.py
@@ -14,7 +14,8 @@
 WMAX = 32
 LANES = 128
 OUT_COPIES = 2
-FETCHES = 2
+ROW_TILES = 8
+FETCHES = 1
 UNIT = 2
 SHARES = (19, 8, 6)
 PIECES = len(SHARES)
@@ -214,11 +215,22 @@
     return rows, value[:, width - LANES :], products[:, width - LANES :]
 
 
+def store_rows(selector, value, rows_ref, skip):
+    trials = rows_ref.shape[0]
+    before = jnp.zeros((value.shape[0], LANES), F32)
+    products = jnp.zeros((selector.shape[0], LANES), F32)
+    for start in range(0, value.shape[1], ROW_TILES * LANES):
+        part = value[:, start : start + ROW_TILES * LANES]
+        rows, before, products = trial_rows(selector, trials, part, before, products)
+        first = max(skip - start, 0)
+        end = start + part.shape[1] - skip
+        rows_ref[:, max(start - skip, 0) : end] = rows[:, first:]
+
+
 def first_rows_kernel(peers, time_all, *refs):
     power_ref, packets, selector_ref = refs[0], refs[1 : 1 + peers], refs[1 + peers]
     rows_ref, scale_ref, line_ref, fold_ref = refs[2 + peers :]
     branches = power_ref.shape[0]
-    trials = rows_ref.shape[0]
     rank = lax.axis_index("tm")
     edge = TAPS - 1
 
@@ -257,8 +269,7 @@
     width = rows_ref.shape[1] - LANES
     value = jnp.concatenate([start, power_ref[:, LANES:width]], axis=1) * scale - 1.0
     value = jnp.concatenate([halo, value], axis=1)
-    nothing = jnp.zeros((selector.shape[0], LANES), F32)
-    rows_ref[...], _, _ = trial_rows(selector, trials, value, jnp.zeros_like(halo), nothing)
+    store_rows(selector, value, rows_ref, 0)
 
 
 def first_rows(power, packets, selector, tiles, time_all):
@@ -283,13 +294,10 @@
 
 
 def more_rows_kernel(start, power_ref, scale_ref, selector_ref, rows_ref):
-    trials, width = rows_ref.shape
+    width = rows_ref.shape[1]
     scale = scale_ref[:, :1]
     value = power_ref[:, start - LANES : start + width] * scale - 1.0
-    selector = selector_ref[...]
-    nothing = jnp.zeros((selector.shape[0], LANES), F32)
-    rows, _, _ = trial_rows(selector, trials, value, jnp.zeros_like(value[:, :LANES]), nothing)
-    rows_ref[...] = rows[:, LANES:]
+    store_rows(selector_ref[...], value, rows_ref, LANES)
 
 
 def more_rows(power, scale, selector, start, tiles):

time: 40.9 us -> 40.9 us (level)
  no operation moved by 1% of the time
where the time goes in v1:
time: 40.9 us; the launch traced here: 40.7 us
  starting transfers between devices  16.3 us (40%)
  waiting for transfers between devices  14.7 us (36%)
  Pallas kernels  8.74 us (21%)
  local copies, waits for them, and re-layouts  0.8 us (2%)
    ppermute x12, starting transfers between devices, swapped(): return lax.ppermute(value, axis, pairs)  16.3 us
    ppermute x12, waiting for transfers between devices, swapped(): return lax.ppermute(value, axis, pairs)  14.7 us
    pallas_call x1, Pallas kernels, channelize(): pl.pallas_call(functools.partial(channel_kernel, pieces), in_specs=[HBM],...  2.39 us
    pallas_call x6, Pallas kernels, merge(): pl.pallas_call(functools.partial(merge_kernel, level, not before), in_spe...  1.45 us
    pallas_call x1, Pallas kernels, finish(): pl.pallas_call(functools.partial(finish_kernel, level), in_specs=[VM] * l...  1.37 us
    pallas_call x2, Pallas kernels, more_rows(): pl.pallas_call(functools.partial(more_rows_kernel, start), in_specs=[VM]...  0.97 us
    pallas_call x2, Pallas kernels, detect(): pl.pallas_call(functools.partial(detect_kernel, level, not before), in_sp...  0.94 us
    pallas_call x1, Pallas kernels, first_rows(): pl.pallas_call(functools.partial(first_rows_kernel, peers, time_all), in_...  0.86 us
  transfers between devices with their start and end apart: 12, of which 8 were waited for; matrix products, arithmetic and copies ran while one was open for 0% of the time, Pallas kernels for 9%

profile of v1, /device:TPU:0, one launch (start us, length us, event | category | flops | bytes accessed | tf_op | source)
XLA Modules:
  0.0 40.7 jit_solution(8382808909854637766)
XLA Ops:
  0.0 0.0 copy-start.2
  0.0 2.4 %channelize.1 = (f32[32,4096]{1,0:T(8,128)S(1)}, f32[8,128]{1,0:T(8,128)S(1)}, f32[40,128]{1,0:T(8,128)S(1)}) custom-call(f32[64,4096]{1,0:T(8,128)} %bitcast.2), custom_call_target="tpu_custom_call" | custom-call | tf_op jit(solution)/shard_map/channelize/pallas_call | solution.py:178
  2.4 2.5 %collective-permute-start.2 = (f32[40,128]{1,0:T(8,128)S(1)}, f32[40,128]{1,0:T(8,128)S(1)}, u32[]{:S(2)}, u32[]{:S(2)}) collective-permute-start(f32[40,128]{1,0:T(8,128)S(1)} %get-tuple-element.25), channel_id=1, source_target_pairs={{0,3},{1,2},{2,1},{3,0},{4,7},{5,6},{6,5},{7,4},{8,11},{9,10},{10,... | collective-permute-start | bytes 61448 | tf_op jit(solution)/shard_map/ppermute | solution.py:37
  4.9 0.7 %collective-permute-start = (f32[40,128]{1,0:T(8,128)S(1)}, f32[40,128]{1,0:T(8,128)S(1)}, u32[]{:S(2)}, u32[]{:S(2)}) collective-permute-start(f32[40,128]{1,0:T(8,128)S(1)} %get-tuple-element.25), channel_id=1, source_target_pairs={{0,1},{1,0},{2,3},{3,2},{4,5},{5,4},{6,7},{7,6},{8,9},{9,8},{10,11... | collective-permute-start | bytes 61448 | tf_op jit(solution)/shard_map/ppermute | solution.py:37
  5.5 0.0 collective-permute-start.1
  5.6 0.0 copy-done.2
  5.6 0.1 copy.6
  5.7 0.0 copy-start
  5.7 0.0 copy-start.1
  5.7 0.7 %copy-done = s32[16,32]{1,0:T(8,128)S(1)} copy-done((s32[16,32]{1,0:T(8,128)S(1)}, s32[16,32]{1,0:T(8,128)}, u32[]{:S(2)}) %copy-start) | copy-done | bytes 2072
  6.4 0.0 copy-done.1
  6.4 0.8 %tables.1 = (bf16[128,192]{1,0:T(8,128)(2,1)S(1)}, bf16[256,512]{1,0:T(8,128)(2,1)S(1)}, f32[8,128]{1,0:T(8,128)S(1)}, bf16[96,96]{1,0:T(8,128)(2,1)S(1)}, s32[48,128]{1,0:T(8,128)S(1)}) custom-call(s32[4]{0:T(128)S(1)} %copy-done.1, s32[16,32]{1,0:T(8,128)S(1)} %copy-done, f32[16,128]{1,0:T(8,128)S(1)} %pad.4.table_ref, ...), custom_call_target="tpu_custom_call" | custom-call | tf_op jit(solution)/shard_map/tables/pallas_call | solution.py:399
  7.2 2.0 %collective-permute-done.1.refs_3_ = f32[8,128]{1,0:T(8,128)S(1)} collective-permute-done((f32[8,128]{1,0:T(8,128)S(1)}, f32[8,128]{1,0:T(8,128)S(1)}, u32[]{:S(2)}, u32[]{:S(2)}) %collective-permute-start.1) | collective-permute-done | bytes 4128 | tf_op jit(solution)/shard_map/ppermute | solution.py:37
  9.2 0.0 collective-permute-done.2.refs_4_
  9.2 0.0 collective-permute-done.refs_2_
  9.2 0.9 %first_rows.1 = (f32[16,2432]{1,0:T(8,128)S(1)}, f32[32,128]{1,0:T(8,128)S(1)}) custom-call(f32[32,4096]{1,0:T(8,128)S(1)} %get-tuple-element.24.refs_0_.power_ref, f32[8,128]{1,0:T(8,128)S(1)} %get-tuple-element.19.after_ref.refs_1_, f32[40,128]{1,0:T(8,128)S(1)} %collective-permute-done.refs_2_, f32[8,128]{1,0:T(8,128)S(1)} %collective-permute-done.1.refs_3_, ...), custom_call_target="tpu_custom_call" | custom-call | tf_op jit(solution)/shard_map/first_rows/pallas_call | solution.py:279
  10.0 1.6 %collective-permute-start.6 = (f32[16,2432]{1,0:T(8,128)S(1)}, f32[16,2432]{1,0:T(8,128)S(1)}, u32[]{:S(2)}, u32[]{:S(2)}) collective-permute-start(f32[16,2432]{1,0:T(8,128)S(1)} %get-tuple-element.28.refs_4_.refs_2_), channel_id=1, source_target_pairs={{0,4},{4,0},{8,12},{12,8},{16,20},{20,16},{24,28},{28,24},{1,5},{5... | collective-permute-start | bytes 466952 | tf_op jit(solution)/shard_map/ppermute | solution.py:37
  11.6 3.7 %collective-permute-done.6.refs_5_.refs_3_ = f32[16,2432]{1,0:T(8,128)S(1)} collective-permute-done((f32[16,2432]{1,0:T(8,128)S(1)}, f32[16,2432]{1,0:T(8,128)S(1)}, u32[]{:S(2)}, u32[]{:S(2)}) %collective-permute-start.6) | collective-permute-done | bytes 155680 | tf_op jit(solution)/shard_map/ppermute | solution.py:37
  15.3 0.3 merge.9.refs_4_.refs_2_
  15.6 1.6 %collective-permute-start.9 = (f32[16,2432]{1,0:T(8,128)S(1)}, f32[16,2432]{1,0:T(8,128)S(1)}, u32[]{:S(2)}, u32[]{:S(2)}) collective-permute-start(f32[16,2432]{1,0:T(8,128)S(1)} %merge.9.refs_4_.refs_2_), channel_id=1, source_target_pairs={{0,8},{4,12},{8,0},{12,4},{16,24},{20,28},{24,16},{28,20},{1,9},{5... | collective-permute-start | bytes 466952 | tf_op jit(solution)/shard_map/ppermute | solution.py:37
  17.2 0.5 %more_rows.3.refs_4_.refs_2_ = f32[16,1024]{1,0:T(8,128)S(1)} custom-call(f32[32,4096]{1,0:T(8,128)S(1)} %get-tuple-element.24.refs_0_.power_ref, f32[32,128]{1,0:T(8,128)S(1)} %get-tuple-element.27.scale_ref, bf16[128,192]{1,0:T(8,128)(2,1)S(1)} %get-tuple-element.26.refs_5_.selector_ref), custom_call_target="tpu_custom_call" | custom-call | tf_op jit(solution)/shard_map/more_rows/pallas_call | solution.py:305
  17.8 1.6 %collective-permute-start.4 = (f32[16,1024]{1,0:T(8,128)S(1)}, f32[16,1024]{1,0:T(8,128)S(1)}, u32[]{:S(2)}, u32[]{:S(2)}) collective-permute-start(f32[16,1024]{1,0:T(8,128)S(1)} %more_rows.3.refs_4_.refs_2_), channel_id=1, source_target_pairs={{0,4},{4,0},{8,12},{12,8},{16,20},{20,16},{24,28},{28,24},{1,5},{5... | collective-permute-start | bytes 196616 | tf_op jit(solution)/shard_map/ppermute | solution.py:37
  19.3 1.6 %collective-permute-done.9.refs_5_.refs_3_ = f32[16,2432]{1,0:T(8,128)S(1)} collective-permute-done((f32[16,2432]{1,0:T(8,128)S(1)}, f32[16,2432]{1,0:T(8,128)S(1)}, u32[]{:S(2)}, u32[]{:S(2)}) %collective-permute-start.9) | collective-permute-done | bytes 155680 | tf_op jit(solution)/shard_map/ppermute | solution.py:37
  20.9 0.3 merge.11.refs_4_.refs_6_
  21.2 3.3 %collective-permute-start.11 = (f32[16,2432]{1,0:T(8,128)S(1)}, f32[16,2432]{1,0:T(8,128)S(1)}, u32[]{:S(2)}, u32[]{:S(2)}) collective-permute-start(f32[16,2432]{1,0:T(8,128)S(1)} %merge.11.refs_4_.refs_6_), channel_id=1, source_target_pairs={{0,16},{4,20},{8,24},{12,28},{16,0},{20,4},{24,8},{28,12},{1,17},{... | collective-permute-start | bytes 466952 | tf_op jit(solution)/shard_map/ppermute | solution.py:37
  24.5 0.5 %more_rows.2.refs_2_ = f32[16,768]{1,0:T(8,128)S(1)} custom-call(f32[32,4096]{1,0:T(8,128)S(1)} %get-tuple-element.24.refs_0_.power_ref, f32[32,128]{1,0:T(8,128)S(1)} %get-tuple-element.27.scale_ref, bf16[128,192]{1,0:T(8,128)(2,1)S(1)} %get-tuple-element.26.refs_5_.selector_ref), custom_call_target="tpu_custom_call" | custom-call | tf_op jit(solution)/shard_map/more_rows/pallas_call | solution.py:305
  24.9 1.6 %collective-permute-start.3 = (f32[16,768]{1,0:T(8,128)S(1)}, f32[16,768]{1,0:T(8,128)S(1)}, u32[]{:S(2)}, u32[]{:S(2)}) collective-permute-start(f32[16,768]{1,0:T(8,128)S(1)} %more_rows.2.refs_2_), channel_id=1, source_target_pairs={{0,4},{4,0},{8,12},{12,8},{16,20},{20,16},{24,28},{28,24},{1,5},{5... | collective-permute-start | bytes 147464 | tf_op jit(solution)/shard_map/ppermute | solution.py:37
  26.5 0.0 collective-permute-done.4.refs_5_.refs_3_
  26.5 0.2 merge.7.refs_4_.refs_2_
  26.8 1.0 %collective-permute-start.7 = (f32[16,1024]{1,0:T(8,128)S(1)}, f32[16,1024]{1,0:T(8,128)S(1)}, u32[]{:S(2)}, u32[]{:S(2)}) collective-permute-start(f32[16,1024]{1,0:T(8,128)S(1)} %merge.7.refs_4_.refs_2_), channel_id=1, source_target_pairs={{0,8},{4,12},{8,0},{12,4},{16,24},{20,28},{24,16},{28,20},{1,9},{5... | collective-permute-start | bytes 196616 | tf_op jit(solution)/shard_map/ppermute | solution.py:37
  27.8 1.3 %collective-permute-done.3.refs_3_ = f32[16,768]{1,0:T(8,128)S(1)} collective-permute-done((f32[16,768]{1,0:T(8,128)S(1)}, f32[16,768]{1,0:T(8,128)S(1)}, u32[]{:S(2)}, u32[]{:S(2)}) %collective-permute-start.3) | collective-permute-done | bytes 49184 | tf_op jit(solution)/shard_map/ppermute | solution.py:37
  29.1 0.2 merge.6.refs_2_
  29.3 1.0 %collective-permute-start.5 = (f32[16,768]{1,0:T(8,128)S(1)}, f32[16,768]{1,0:T(8,128)S(1)}, u32[]{:S(2)}, u32[]{:S(2)}) collective-permute-start(f32[16,768]{1,0:T(8,128)S(1)} %merge.6.refs_2_), channel_id=1, source_target_pairs={{0,8},{4,12},{8,0},{12,4},{16,24},{20,28},{24,16},{28,20},{1,9},{5... | collective-permute-start | bytes 147464 | tf_op jit(solution)/shard_map/ppermute | solution.py:37
  30.3 0.7 %collective-permute-done.7.refs_5_.refs_3_ = f32[16,1024]{1,0:T(8,128)S(1)} collective-permute-done((f32[16,1024]{1,0:T(8,128)S(1)}, f32[16,1024]{1,0:T(8,128)S(1)}, u32[]{:S(2)}, u32[]{:S(2)}) %collective-permute-start.7) | collective-permute-done | bytes 65568 | tf_op jit(solution)/shard_map/ppermute | solution.py:37
  31.1 0.2 merge.10.refs_4_.refs_6_
  31.3 0.5 %collective-permute-start.10 = (f32[16,1024]{1,0:T(8,128)S(1)}, f32[16,1024]{1,0:T(8,128)S(1)}, u32[]{:S(2)}, u32[]{:S(2)}) collective-permute-start(f32[16,1024]{1,0:T(8,128)S(1)} %merge.10.refs_4_.refs_6_), channel_id=1, source_target_pairs={{0,16},{4,20},{8,24},{12,28},{16,0},{20,4},{24,8},{28,12},{1,17},{... | collective-permute-start | bytes 196616 | tf_op jit(solution)/shard_map/ppermute | solution.py:37
  31.8 1.7 %collective-permute-done.5.refs_3_ = f32[16,768]{1,0:T(8,128)S(1)} collective-permute-done((f32[16,768]{1,0:T(8,128)S(1)}, f32[16,768]{1,0:T(8,128)S(1)}, u32[]{:S(2)}, u32[]{:S(2)}) %collective-permute-start.5) | collective-permute-done | bytes 49184 | tf_op jit(solution)/shard_map/ppermute | solution.py:37
  33.5 0.2 merge.8.refs_4_
  33.7 0.9 %collective-permute-start.8 = (f32[16,768]{1,0:T(8,128)S(1)}, f32[16,768]{1,0:T(8,128)S(1)}, u32[]{:S(2)}, u32[]{:S(2)}) collective-permute-start(f32[16,768]{1,0:T(8,128)S(1)} %merge.8.refs_4_), channel_id=1, source_target_pairs={{0,16},{4,20},{8,24},{12,28},{16,0},{20,4},{24,8},{28,12},{1,17},{... | collective-permute-start | bytes 147464 | tf_op jit(solution)/shard_map/ppermute | solution.py:37
  34.6 0.0 collective-permute-done.11.refs_5_.refs_7_
  34.6 0.5 %detect.2 = (f32[16,2432]{1,0:T(8,128)S(1)}, f32[4,16,2304]{2,1,0:T(8,128)S(1)}) custom-call(bf16[96,96]{1,0:T(8,128)(2,1)S(1)} %get-tuple-element.20.refs_0_, s32[48,128]{1,0:T(8,128)S(1)} %get-tuple-element.21.refs_1_, bf16[256,512]{1,0:T(8,128)(2,1)S(1)} %get-tuple-element.22.refs_2_, f32[8,128]{1,0:T(8,128)S(1)} %get-tuple-element.23.refs_3_, ...), custom_call_target="tpu_custom_call" | custom-call | tf_op jit(solution)/shard_map/detect/pallas_call | solution.py:447
  35.1 1.4 %collective-permute-done.10.refs_5_.refs_7_ = f32[16,1024]{1,0:T(8,128)S(1)} collective-permute-done((f32[16,1024]{1,0:T(8,128)S(1)}, f32[16,1024]{1,0:T(8,128)S(1)}, u32[]{:S(2)}, u32[]{:S(2)}) %collective-permute-start.10) | collective-permute-done | bytes 65568 | tf_op jit(solution)/shard_map/ppermute | solution.py:37
  36.6 0.4 %detect.3 = (f32[16,1024]{1,0:T(8,128)S(1)}, f32[4,16,1024]{2,1,0:T(8,128)S(1)}) custom-call(bf16[96,96]{1,0:T(8,128)(2,1)S(1)} %get-tuple-element.20.refs_0_, s32[48,128]{1,0:T(8,128)S(1)} %get-tuple-element.21.refs_1_, bf16[256,512]{1,0:T(8,128)(2,1)S(1)} %get-tuple-element.22.refs_2_, f32[8,128]{1,0:T(8,128)S(1)} %get-tuple-element.23.refs_3_, ...), custom_call_target="tpu_custom_call" | custom-call | tf_op jit(solution)/shard_map/detect/pallas_call | solution.py:447
  37.0 2.3 %collective-permute-done.8.refs_5_ = f32[16,768]{1,0:T(8,128)S(1)} collective-permute-done((f32[16,768]{1,0:T(8,128)S(1)}, f32[16,768]{1,0:T(8,128)S(1)}, u32[]{:S(2)}, u32[]{:S(2)}) %collective-permute-start.8) | collective-permute-done | bytes 49184 | tf_op jit(solution)/shard_map/ppermute | solution.py:37
  39.3 1.4 %finish.1 = f32[16,4,4096]{2,1,0:T(4,128)} custom-call(bf16[96,96]{1,0:T(8,128)(2,1)S(1)} %get-tuple-element.20.refs_0_, s32[48,128]{1,0:T(8,128)S(1)} %get-tuple-element.21.refs_1_, bf16[256,512]{1,0:T(8,128)(2,1)S(1)} %get-tuple-element.22.refs_2_, f32[8,128]{1,0:T(8,128)S(1)} %get-tuple-element.23.refs_3_, f32[16,768]{1,0:T(8,128)S(1)} %merge.8.refs_4_, ...), custom_call_target="tpu_custom_call" | custom-call | tf_op jit(solution)/shard_map/finish/pallas_call | solution.py:500
  (3 shorter events, 0.0 us)
Async XLA Ops:
  0.0 5.6 %copy-start.2 = (s32[3,3,16]{2,1,0:T(4,128)S(1)}, s32[3,3,16]{2,1,0:T(4,128)}, u32[]{:S(2)}) copy-start(s32[3,3,16]{2,1,0:T(4,128)} %param.6) | copy-start | bytes 1732
  2.4 6.8 %collective-permute-start.2 = (f32[40,128]{1,0:T(8,128)S(1)}, f32[40,128]{1,0:T(8,128)S(1)}, u32[]{:S(2)}, u32[]{:S(2)}) collective-permute-start(f32[40,128]{1,0:T(8,128)S(1)} %get-tuple-element.25), channel_id=1, source_target_pairs={{0,3},{1,2},{2,1},{3,0},{4,7},{5,6},{6,5},{7,4},{8,11},{9,10},{10,... | collective-permute-start | bytes 61448 | tf_op jit(solution)/shard_map/ppermute | solution.py:37
  4.9 4.3 %collective-permute-start = (f32[40,128]{1,0:T(8,128)S(1)}, f32[40,128]{1,0:T(8,128)S(1)}, u32[]{:S(2)}, u32[]{:S(2)}) collective-permute-start(f32[40,128]{1,0:T(8,128)S(1)} %get-tuple-element.25), channel_id=1, source_target_pairs={{0,1},{1,0},{2,3},{3,2},{4,5},{5,4},{6,7},{7,6},{8,9},{9,8},{10,11... | collective-permute-start | bytes 61448 | tf_op jit(solution)/shard_map/ppermute | solution.py:37
  5.5 3.6 %collective-permute-start.1 = (f32[8,128]{1,0:T(8,128)S(1)}, f32[8,128]{1,0:T(8,128)S(1)}, u32[]{:S(2)}, u32[]{:S(2)}) collective-permute-start(f32[8,128]{1,0:T(8,128)S(1)} %get-tuple-element.19.after_ref.refs_1_), channel_id=1, source_target_pairs={{0,2},{1,3},{2,0},{3,1},{4,6},{5,7},{6,4},{7,5},{8,10},{9,11},{10,... | collective-permute-start | bytes 12296 | tf_op jit(solution)/shard_map/ppermute | solution.py:37
  5.7 0.7 %copy-start = (s32[16,32]{1,0:T(8,128)S(1)}, s32[16,32]{1,0:T(8,128)}, u32[]{:S(2)}) copy-start(s32[16,32]{1,0:T(8,128)} %delay_ref.1) | copy-start | bytes 6148
  5.7 0.7 %copy-start.1 = (s32[4]{0:T(128)S(1)}, s32[4]{0:T(128)}, u32[]{:S(2)}) copy-start(s32[4]{0:T(128)} %width_ref.1) | copy-start | bytes 52
  10.0 5.3 %collective-permute-start.6 = (f32[16,2432]{1,0:T(8,128)S(1)}, f32[16,2432]{1,0:T(8,128)S(1)}, u32[]{:S(2)}, u32[]{:S(2)}) collective-permute-start(f32[16,2432]{1,0:T(8,128)S(1)} %get-tuple-element.28.refs_4_.refs_2_), channel_id=1, source_target_pairs={{0,4},{4,0},{8,12},{12,8},{16,20},{20,16},{24,28},{28,24},{1,5},{5... | collective-permute-start | bytes 466952 | tf_op jit(solution)/shard_map/ppermute | solution.py:37
  15.6 5.3 %collective-permute-start.9 = (f32[16,2432]{1,0:T(8,128)S(1)}, f32[16,2432]{1,0:T(8,128)S(1)}, u32[]{:S(2)}, u32[]{:S(2)}) collective-permute-start(f32[16,2432]{1,0:T(8,128)S(1)} %merge.9.refs_4_.refs_2_), channel_id=1, source_target_pairs={{0,8},{4,12},{8,0},{12,4},{16,24},{20,28},{24,16},{28,20},{1,9},{5... | collective-permute-start | bytes 466952 | tf_op jit(solution)/shard_map/ppermute | solution.py:37
  17.8 8.8 %collective-permute-start.4 = (f32[16,1024]{1,0:T(8,128)S(1)}, f32[16,1024]{1,0:T(8,128)S(1)}, u32[]{:S(2)}, u32[]{:S(2)}) collective-permute-start(f32[16,1024]{1,0:T(8,128)S(1)} %more_rows.3.refs_4_.refs_2_), channel_id=1, source_target_pairs={{0,4},{4,0},{8,12},{12,8},{16,20},{20,16},{24,28},{28,24},{1,5},{5... | collective-permute-start | bytes 196616 | tf_op jit(solution)/shard_map/ppermute | solution.py:37
  21.2 13.4 %collective-permute-start.11 = (f32[16,2432]{1,0:T(8,128)S(1)}, f32[16,2432]{1,0:T(8,128)S(1)}, u32[]{:S(2)}, u32[]{:S(2)}) collective-permute-start(f32[16,2432]{1,0:T(8,128)S(1)} %merge.11.refs_4_.refs_6_), channel_id=1, source_target_pairs={{0,16},{4,20},{8,24},{12,28},{16,0},{20,4},{24,8},{28,12},{1,17},{... | collective-permute-start | bytes 466952 | tf_op jit(solution)/shard_map/ppermute | solution.py:37
  24.9 4.2 %collective-permute-start.3 = (f32[16,768]{1,0:T(8,128)S(1)}, f32[16,768]{1,0:T(8,128)S(1)}, u32[]{:S(2)}, u32[]{:S(2)}) collective-permute-start(f32[16,768]{1,0:T(8,128)S(1)} %more_rows.2.refs_2_), channel_id=1, source_target_pairs={{0,4},{4,0},{8,12},{12,8},{16,20},{20,16},{24,28},{28,24},{1,5},{5... | collective-permute-start | bytes 147464 | tf_op jit(solution)/shard_map/ppermute | solution.py:37
  26.8 4.3 %collective-permute-start.7 = (f32[16,1024]{1,0:T(8,128)S(1)}, f32[16,1024]{1,0:T(8,128)S(1)}, u32[]{:S(2)}, u32[]{:S(2)}) collective-permute-start(f32[16,1024]{1,0:T(8,128)S(1)} %merge.7.refs_4_.refs_2_), channel_id=1, source_target_pairs={{0,8},{4,12},{8,0},{12,4},{16,24},{20,28},{24,16},{28,20},{1,9},{5... | collective-permute-start | bytes 196616 | tf_op jit(solution)/shard_map/ppermute | solution.py:37
  29.3 4.2 %collective-permute-start.5 = (f32[16,768]{1,0:T(8,128)S(1)}, f32[16,768]{1,0:T(8,128)S(1)}, u32[]{:S(2)}, u32[]{:S(2)}) collective-permute-start(f32[16,768]{1,0:T(8,128)S(1)} %merge.6.refs_2_), channel_id=1, source_target_pairs={{0,8},{4,12},{8,0},{12,4},{16,24},{20,28},{24,16},{28,20},{1,9},{5... | collective-permute-start | bytes 147464 | tf_op jit(solution)/shard_map/ppermute | solution.py:37
  31.3 5.2 %collective-permute-start.10 = (f32[16,1024]{1,0:T(8,128)S(1)}, f32[16,1024]{1,0:T(8,128)S(1)}, u32[]{:S(2)}, u32[]{:S(2)}) collective-permute-start(f32[16,1024]{1,0:T(8,128)S(1)} %merge.10.refs_4_.refs_6_), channel_id=1, source_target_pairs={{0,16},{4,20},{8,24},{12,28},{16,0},{20,4},{24,8},{28,12},{1,17},{... | collective-permute-start | bytes 196616 | tf_op jit(solution)/shard_map/ppermute | solution.py:37
  33.7 5.6 %collective-permute-start.8 = (f32[16,768]{1,0:T(8,128)S(1)}, f32[16,768]{1,0:T(8,128)S(1)}, u32[]{:S(2)}, u32[]{:S(2)}) collective-permute-start(f32[16,768]{1,0:T(8,128)S(1)} %merge.8.refs_4_), channel_id=1, source_target_pairs={{0,16},{4,20},{8,24},{12,28},{16,0},{20,4},{24,8},{28,12},{1,17},{... | collective-permute-start | bytes 147464 | tf_op jit(solution)/shard_map/ppermute | solution.py:37
